TPU v7x, 512 devices: a whole 4x8x8 slice. The times are simulated.
512 devices in a mesh: head: 4 (over x), blk: 128 (over y, z, core).
Axes of the slice: x: 4, y: 8, z: 8, core: 2. Of those that a mesh axis runs over, the one named last changes fastest.
Arguments:
- tokens: bfloat16 [8192, 2048], P('blk'), may hold values from -6 to 6
- q_weight: bfloat16 [2048, 1024], P(None, 'head')
- k_weight: bfloat16 [2048, 256], P(None, 'head')
- v_weight: bfloat16 [2048, 256], P(None, 'head'), may hold values from -0.125 to 0.125
- o_weight: bfloat16 [1024, 2048], P('head'), may hold values from -0.1875 to 0.1875
- kv_pages: bfloat16 [4, 384, 64, 128], P('head', 'blk')
- page_node: int32 [384], replicated, may hold values from 0 to 72, as said below
- page_fill: int32 [384], replicated, may hold values from 1 to 64
- req_len: int32 [64], replicated, may hold values from 1 to 256, 8192 in all
- req_leaf: int32 [64], replicated, may hold values from 0 to 63
- leaf_parent: int32 [64], replicated, may hold values from 0 to 7
Outputs:
- attn_out: bfloat16 [8192, 2048], P('blk', 'head')
Inputs may be any that keep to these rules, and one draw needn't show every extreme that they name: `req_len`: their sum is 8192, and the longest request has exactly 256 tokens. `page_node`: node 0 is the root, nodes 1 to 8 form the middle level and the rest are leaves; the root holds a third of the 384 pages, each middle node a 1 / 8 share of another third, each leaf two pages, placed over the pages in any order.
All inputs are finite; a program needn't handle non-finite values.
Results may differ from a plain program's by a relative error of at most 0.012.
The roundings to bfloat16 on the way count: a program that leaves them out, or rounds other values in their place, can miss the bound.
Values may be sent and summed in bfloat16 or wider, within the bound.
A program may use at most 128 MiB of HBM per device.

v0:
```python
import jax
import jax.numpy as jnp
from jax import lax
from jax.sharding import PartitionSpec as P

HD = 64
MIDS = 8
PROMPT = 256
NEGATIVE = -1e30
EPSILON = 1e-06
ROPE_BASE = 10000.0
SCORE_SCALE = 0.125


def shifted(value, axis, steps):
    count = lax.axis_size(axis)
    first, last = (max(0, -steps), min(count, count - steps))
    return lax.ppermute(value, axis, [(source, source + steps) for source in range(first, last)])


def norm_rows(hidden):
    wide = hidden.astype(jnp.float32)
    return (wide * lax.rsqrt(jnp.mean(wide * wide, axis=-1, keepdims=True) + EPSILON)).astype(
        jnp.bfloat16
    )


def rotate(values, positions):
    half_dim = values.shape[-1] // 2
    frequency = ROPE_BASE ** (-jnp.arange(half_dim).astype(jnp.float32) / half_dim)
    angles = positions.astype(jnp.float32)[:, None] * frequency[None, :]
    cosine = jnp.cos(angles)[:, None, :]
    sine_part = jnp.sin(angles)[:, None, :]
    first_half = values[..., :half_dim]
    second = values[..., half_dim:]
    return jnp.concatenate(
        [first_half * cosine - second * sine_part, second * cosine + first_half * sine_part],
        axis=-1,
    )


def request_of(places, req_len):
    req_end = jnp.cumsum(req_len)
    return jnp.sum((places[:, None] >= req_end[None, :]).astype(jnp.int32), axis=1)


def row_paths(places, req_len, req_leaf, leaf_parent, page_node, page_fill):
    req_count = req_len.shape[0]
    leaf_count = leaf_parent.shape[0]
    node_count = 1 + MIDS + leaf_count
    starts = jnp.cumsum(req_len) - req_len
    request = request_of(places, req_len)
    chosen = request[:, None] == jnp.arange(req_count, dtype=jnp.int32)[None, :]
    offset = places - jnp.sum(jnp.where(chosen, starts[None, :], 0), axis=1)
    leaf_id = jnp.sum(jnp.where(chosen, req_leaf[None, :], 0), axis=1)
    leaf_hit = leaf_id[:, None] == jnp.arange(leaf_count, dtype=jnp.int32)[None, :]
    mid_id = jnp.sum(jnp.where(leaf_hit, leaf_parent[None, :], 0), axis=1)
    path_ids = jnp.stack([jnp.zeros_like(mid_id), 1 + mid_id, 1 + MIDS + leaf_id], axis=1)
    node_hit = page_node[:, None] == jnp.arange(node_count, dtype=jnp.int32)[None, :]
    node_len = jnp.sum(jnp.where(node_hit, page_fill[:, None], 0), axis=0)
    on_path = path_ids[:, :, None] == jnp.arange(node_count, dtype=jnp.int32)[None, None, :]
    prefix = jnp.sum(jnp.where(on_path, node_len[None, None, :], 0), axis=(1, 2))
    return (request, path_ids, prefix + offset)


def page_mask(path_ids, nodes_here, fills_here, page_len):
    node_hit = jnp.any(path_ids[:, :, None] == nodes_here[None, None, :], axis=1)
    slot_live = jnp.arange(page_len, dtype=jnp.int32)[None, :] < fills_here[:, None]
    return (node_hit[:, :, None] & slot_live[None, :, :]).reshape(path_ids.shape[0], -1)


def block_size(total_pages, page_limit):
    chosen = 1
    for trial_size in range(1, min(total_pages, page_limit) + 1):
        if total_pages % trial_size == 0:
            chosen = trial_size
    return chosen


def fold_keys(running, q_rot, key_rows, values, allowed):
    top_old, total_old, accum_old = running
    scores = (
        jnp.einsum("rkhd,knd->khrn", q_rot, key_rows, preferred_element_type=jnp.float32)
        * SCORE_SCALE
    )
    scores = jnp.where(allowed[None, None], scores, NEGATIVE)
    top_new = jnp.maximum(top_old, jnp.max(scores, axis=-1))
    weights = jnp.where(allowed[None, None], jnp.exp(scores - top_new[..., None]), 0.0)
    factor = jnp.exp(top_old - top_new)
    total_new = total_old * factor + jnp.sum(weights, axis=-1)
    product = jnp.einsum(
        "khrn,knd->khrd", weights.astype(jnp.bfloat16), values, preferred_element_type=jnp.float32
    )
    return (top_new, total_new, accum_old * factor[..., None] + product)


def local(
    tokens,
    q_weight,
    k_weight,
    v_weight,
    o_weight,
    kv_pages,
    page_node,
    page_fill,
    req_len,
    req_leaf,
    leaf_parent,
):
    local_rows = tokens.shape[0]
    kv_heads = k_weight.shape[1] // HD
    q_heads = q_weight.shape[1] // HD
    group_size = q_heads // kv_heads
    page_len = kv_pages.shape[2]
    blk_index = lax.axis_index("blk")
    places = blk_index * local_rows + jnp.arange(local_rows, dtype=jnp.int32)
    request, path_ids, positions = row_paths(
        places, req_len, req_leaf, leaf_parent, page_node, page_fill
    )
    normed = norm_rows(tokens)
    queries = jnp.dot(normed, q_weight, preferred_element_type=jnp.float32).reshape(
        local_rows, q_heads, HD
    )
    q_rot = (
        rotate(queries, positions)
        .astype(jnp.bfloat16)
        .reshape(local_rows, kv_heads, group_size, HD)
    )
    keys_new = jnp.dot(normed, k_weight, preferred_element_type=jnp.float32).reshape(
        local_rows, kv_heads, HD
    )
    keys_new = rotate(keys_new, positions).astype(jnp.bfloat16)
    values_new = (
        jnp.dot(normed, v_weight, preferred_element_type=jnp.float32)
        .astype(jnp.bfloat16)
        .reshape(local_rows, kv_heads, HD)
    )
    own_pack = jnp.concatenate([keys_new, values_new], axis=-1)
    reach_devs = (PROMPT - 1) // local_rows + 1
    near_packs = [own_pack]
    near_places = [places]
    for distance in range(1, reach_devs + 1):
        near_packs.insert(0, shifted(own_pack, "blk", distance))
        near_places.insert(0, places - distance * local_rows)
    near_pack = jnp.swapaxes(jnp.concatenate(near_packs, axis=0), 0, 1)
    near_place = jnp.concatenate(near_places)
    near_req = request_of(jnp.maximum(near_place, 0), req_len)
    near_ok = (
        (near_place[None, :] >= 0)
        & (near_req[None, :] == request[:, None])
        & (near_place[None, :] <= places[:, None])
    )
    start_state = (
        jnp.full((kv_heads, group_size, local_rows), NEGATIVE, jnp.float32),
        jnp.zeros((kv_heads, group_size, local_rows), jnp.float32),
        jnp.zeros((kv_heads, group_size, local_rows, HD), jnp.float32),
    )
    running = fold_keys(start_state, q_rot, near_pack[..., :HD], near_pack[..., HD:], near_ok)
    group_limit = max(1, 2048 // page_len)
    shard_pages = lax.all_gather(kv_pages, "blk", axis=1, tiled=True)
    page_total = shard_pages.shape[1]
    group_pages = block_size(page_total, group_limit)

    def one_group(group_index, inner):
        first_page = group_index * group_pages
        page_block = lax.dynamic_slice_in_dim(shard_pages, first_page, group_pages, 1)
        nodes_here = lax.dynamic_slice_in_dim(page_node, first_page, group_pages, 0)
        fills_here = lax.dynamic_slice_in_dim(page_fill, first_page, group_pages, 0)
        allowed = page_mask(path_ids, nodes_here, fills_here, page_len)
        flat_block = page_block.reshape(kv_heads, group_pages * page_len, 2 * HD)
        return fold_keys(inner, q_rot, flat_block[..., :HD], flat_block[..., HD:], allowed)

    running = lax.fori_loop(0, page_total // group_pages, one_group, running)
    top_all, total_all, accum_all = running
    attended = accum_all / total_all[..., None]
    attended = (
        jnp.transpose(attended, (2, 0, 1, 3)).reshape(local_rows, q_heads * HD).astype(jnp.bfloat16)
    )
    partial_out = jnp.dot(attended, o_weight, preferred_element_type=jnp.float32)
    return lax.psum_scatter(partial_out, "head", scatter_dimension=1, tiled=True).astype(
        jnp.bfloat16
    )


def solution(mesh):
    return jax.shard_map(
        local,
        mesh=mesh,
        in_specs=(
            P("blk", None),
            P(None, "head"),
            P(None, "head"),
            P(None, "head"),
            P("head", None),
            P("head", "blk", None, None),
            P(),
            P(),
            P(),
            P(),
            P(),
        ),
        out_specs=P("blk", "head"),
        check_vma=False,
    )
```

profile of v0, /device:TPU:8, one launch (start us, length us, event | category | flops | bytes accessed | tf_op | source)
XLA Modules:
  0.0 205.3 jit_solution(11109464322911127699)
XLA Ops:
  11.9 1.1 fusion.17
  13.1 1.3 convolution_bitcast_fusion.1
  14.8 1.3 fusion.16
  16.2 1.9 collective-permute-start.3
  18.1 4.3 %collective-permute-start.2 = (bf16[64,1,128]{2,0,1:T(8,128)(2,1)S(1)}, bf16[64,1,128]{2,0,1:T(8,128)(2,1)S(1)}, u32[]{:S(2)}, u32[]{:S(2)}) collective-permute-start(bf16[64,1,128]{2,0,1:T(8,128)(2,1)S(1)} %pad_maximum_fusion.1), channel_id=1, source_target_pairs={{0,2},{1,3},{2,4},{3,5},{4,6},{5,7},{6,8},{7,9},{8,10},{9,11},{10,... | collective-permute-start | bytes 49160 | tf_op jit(solution)/shard_map/ppermute | solution.py:18
  22.4 6.1 %collective-permute-start.1 = (bf16[64,1,128]{2,0,1:T(8,128)(2,1)S(1)}, bf16[64,1,128]{2,0,1:T(8,128)(2,1)S(1)}, u32[]{:S(2)}, u32[]{:S(2)}) collective-permute-start(bf16[64,1,128]{2,0,1:T(8,128)(2,1)S(1)} %pad_maximum_fusion.1), channel_id=1, source_target_pairs={{0,3},{1,4},{2,5},{3,6},{4,7},{5,8},{6,9},{7,10},{8,11},{9,12},{10... | collective-permute-start | bytes 49160 | tf_op jit(solution)/shard_map/ppermute | solution.py:18
  28.5 6.4 %collective-permute-start = (bf16[64,1,128]{2,0,1:T(8,128)(2,1)S(1)}, bf16[64,1,128]{2,0,1:T(8,128)(2,1)S(1)}, u32[]{:S(2)}, u32[]{:S(2)}) collective-permute-start(bf16[64,1,128]{2,0,1:T(8,128)(2,1)S(1)} %pad_maximum_fusion.1), channel_id=1, source_target_pairs={{0,4},{1,5},{2,6},{3,7},{4,8},{5,9},{6,10},{7,11},{8,12},{9,13},{1... | collective-permute-start | bytes 49160 | tf_op jit(solution)/shard_map/ppermute | solution.py:18
  34.9 1.7 fusion.41
  38.5 62.9 %all-gather.2.cloned.1.call-done = bf16[1,384,64,128]{3,2,0,1:T(8,128)(2,1)} async-done(((bf16[1,3,64,128]{3,2,0,1:T(8,128)(2,1)}), bf16[1,384,64,128]{3,2,0,1:T(8,128)(2,1)}) %all-gather.2.cloned.1.call-update) | async-done | bytes 6291472 | tf_op jit(solution)/shard_map/all_gather | solution.py:160
  101.3 70.1 %while.17 = (s32[]{:T(128)}, f32[1,4,64]{2,1,0:T(4,128)S(1)}, f32[1,4,64]{2,1,0:T(4,128)S(1)}, f32[1,4,64,64]{3,2,1,0:T(8,128)S(1)}, s32[64,3]{0,1:T(4,128)S(1)}...) while((s32[]{:T(128)}, f32[1,4,64]{2,1,0:T(4,128)S(1)}, ...), condition=%wide.region_15.16_spmd, body=%wide.region_11.15_spmd.sunk | while | flops 139113216 | bytes 9696951 | solution.py:173
  104.2 1.1 constant_dynamic-slice_fusion.2
  110.1 1.1 constant_dynamic-slice_fusion.2
  115.9 1.1 constant_dynamic-slice_fusion.2
  121.8 1.1 constant_dynamic-slice_fusion.2
  127.6 1.1 constant_dynamic-slice_fusion.2
  133.4 1.1 constant_dynamic-slice_fusion.2
  139.3 1.1 constant_dynamic-slice_fusion.2
  151.0 1.1 constant_dynamic-slice_fusion.2
  156.8 1.1 constant_dynamic-slice_fusion.2
  162.7 1.1 constant_dynamic-slice_fusion.2
  168.5 1.1 constant_dynamic-slice_fusion.2
  171.7 1.1 fusion.48
  172.8 24.0 %reduce-scatter.2.cloned.1.call-done = f32[64,512]{1,0:T(8,128)} async-done(((f32[64,2048]{1,0:T(8,128)}), f32[64,512]{1,0:T(8,128)}) %reduce-scatter.2.cloned.1.call-update) | async-done | bytes 131088 | tf_op jit(solution)/shard_map/reduce_scatter | solution.py:180
  196.9 1.5 convert_element_type.84
  (273 shorter events, 65.2 us)
Async XLA Ops:
  6.5 165.2 %copy-start = (bf16[256,2048]{1,0:T(8,128)(2,1)S(1)}, bf16[256,2048]{1,0:T(8,128)(2,1)}, u32[]{:S(2)}) copy-start(bf16[256,2048]{1,0:T(8,128)(2,1)} %param.17) | copy-start | bytes 3145732
  6.5 94.8 %all-gather.2.cloned.1.call-start = ((), (), s32[]{:S(2)}) async-start(), calls=%async_computation.1 | async-start | bytes 6340608 | tf_op jit(solution)/shard_map/all_gather | solution.py:160
  7.3 189.6 %reduce-scatter.2.cloned.1.call-start = ((), (), s32[]{:S(2)}) async-start(), calls=%async_computation.2 | async-start | bytes 655360 | tf_op jit(solution)/shard_map/reduce_scatter | solution.py:180
  16.2 21.4 %collective-permute-start.3 = (bf16[64,1,128]{2,0,1:T(8,128)(2,1)S(1)}, bf16[64,1,128]{2,0,1:T(8,128)(2,1)S(1)}, u32[]{:S(2)}, u32[]{:S(2)}) collective-permute-start(bf16[64,1,128]{2,0,1:T(8,128)(2,1)S(1)} %pad_maximum_fusion.1), channel_id=1, source_target_pairs={{0,1},{1,2},{2,3},{3,4},{4,5},{5,6},{6,7},{7,8},{8,9},{9,10},{10,1... | collective-permute-start | bytes 49160 | tf_op jit(solution)/shard_map/ppermute | solution.py:18
  18.1 19.4 %collective-permute-start.2 = (bf16[64,1,128]{2,0,1:T(8,128)(2,1)S(1)}, bf16[64,1,128]{2,0,1:T(8,128)(2,1)S(1)}, u32[]{:S(2)}, u32[]{:S(2)}) collective-permute-start(bf16[64,1,128]{2,0,1:T(8,128)(2,1)S(1)} %pad_maximum_fusion.1), channel_id=1, source_target_pairs={{0,2},{1,3},{2,4},{3,5},{4,6},{5,7},{6,8},{7,9},{8,10},{9,11},{10,... | collective-permute-start | bytes 49160 | tf_op jit(solution)/shard_map/ppermute | solution.py:18
  22.4 15.1 %collective-permute-start.1 = (bf16[64,1,128]{2,0,1:T(8,128)(2,1)S(1)}, bf16[64,1,128]{2,0,1:T(8,128)(2,1)S(1)}, u32[]{:S(2)}, u32[]{:S(2)}) collective-permute-start(bf16[64,1,128]{2,0,1:T(8,128)(2,1)S(1)} %pad_maximum_fusion.1), channel_id=1, source_target_pairs={{0,3},{1,4},{2,5},{3,6},{4,7},{5,8},{6,9},{7,10},{8,11},{9,12},{10... | collective-permute-start | bytes 49160 | tf_op jit(solution)/shard_map/ppermute | solution.py:18
  28.5 9.0 %collective-permute-start = (bf16[64,1,128]{2,0,1:T(8,128)(2,1)S(1)}, bf16[64,1,128]{2,0,1:T(8,128)(2,1)S(1)}, u32[]{:S(2)}, u32[]{:S(2)}) collective-permute-start(bf16[64,1,128]{2,0,1:T(8,128)(2,1)S(1)} %pad_maximum_fusion.1), channel_id=1, source_target_pairs={{0,4},{1,5},{2,6},{3,7},{4,8},{5,9},{6,10},{7,11},{8,12},{9,13},{1... | collective-permute-start | bytes 49160 | tf_op jit(solution)/shard_map/ppermute | solution.py:18
Sparse Core Ops, SparseCore 0:
  10.5 90.7 all-gather.1
  173.0 23.8 reduce-scatter.1
where the time goes:
time: 207 us; the launch traced here: 205 us
  waiting for transfers between devices  87.6 us (42%)
  local copies, waits for them, and re-layouts  47 us (23%)
  matrix products  21.1 us (10%)
  starting transfers between devices  18.7 us (9%)
  other arithmetic  16.3 us (8%)
  between operations  13.7 us (7%)
    all_gather x1, waiting for transfers between devices, local(): shard_pages = lax.all_gather(kv_pages, 'blk', axis=1, tiled=True)  62.9 us
    reduce_scatter x1, waiting for transfers between devices, local(): lax.psum_scatter(partial_out, 'head', scatter_dimension=1, tiled=True)  24 us
    ppermute x4, starting transfers between devices, shifted(): lax.ppermute(value, axis, [(source, source + steps) for source in range(f...  18.7 us
    dynamic_slice x12, local copies, waits for them, and re-layouts, one_group(): lax.dynamic_slice_in_dim(shard_pages, first_page, group_pages, 1)  13 us
    and x24, local copies, waits for them, and re-layouts, page_mask(): node_hit[:, :, None] & slot_live[None, :, :]  9.91 us
    dynamic_slice x12, local copies, waits for them, and re-layouts, one_group(): fills_here = lax.dynamic_slice_in_dim(page_fill, first_page, group_pages, 0)  9.1 us
    dynamic_slice x12, local copies, waits for them, and re-layouts, one_group(): nodes_here = lax.dynamic_slice_in_dim(page_node, first_page, group_pages, 0)  9.04 us
    dot_general x13, matrix products, fold_keys(): jnp.einsum('khrn,knd->khrd', weights.astype(jnp.bfloat16), values, prefer...  8.63 us
  transfers between devices with their start and end apart: 6, of which 2 were waited for; matrix products, arithmetic and copies ran while one was open for 6% of the time, Pallas kernels for 0%

commit v1 on v0

--- a/solution.py
+++ b/solution.py
@@ -157,7 +157,9 @@
     )
     running = fold_keys(start_state, q_rot, near_pack[..., :HD], near_pack[..., HD:], near_ok)
     group_limit = max(1, 2048 // page_len)
-    shard_pages = lax.all_gather(kv_pages, "blk", axis=1, tiled=True)
+    shard_pages = jnp.concatenate(
+        lax.all_to_all(jnp.stack([kv_pages] * lax.axis_size("blk")), "blk", 0, 0), axis=1
+    )
     page_total = shard_pages.shape[1]
     group_pages = block_size(page_total, group_limit)
 

time: 207 us -> 303 us (1.46)
  waiting for transfers between devices: 87.6 us -> 189 us
  starting transfers between devices: 18.7 us -> 32 us
  local copies, waits for them, and re-layouts: 47 us -> 35.2 us
  other arithmetic: 16.3 us -> 12.7 us
  matrix products: 21.1 us -> 17.8 us
    ppermute x4, waiting for transfers between devices: 0.01 us -> 137 us  [shifted(): lax.ppermute(value, axis, [(source, source + steps) for source in range(f...]
    all_gather x1 -> x0, waiting for transfers between devices: 62.9 us -> none  [local(): shard_pages = lax.all_gather(kv_pages, 'blk', axis=1, tiled=True)]
    reduce_scatter x1, waiting for transfers between devices: 24 us -> 51.7 us  [local(): lax.psum_scatter(partial_out, 'head', scatter_dimension=1, tiled=True)]
    all_to_all x0 -> x1, starting transfers between devices: none -> 17.9 us  [local(): lax.all_to_all(jnp.stack([kv_pages] * lax.axis_size('blk')), 'blk', 0, 0)]
    dynamic_slice x12, local copies, waits for them, and re-layouts: 9.1 us -> 0.95 us  [one_group(): fills_here = lax.dynamic_slice_in_dim(page_fill, first_page, group_pages, 0)]
    dynamic_slice x12, local copies, waits for them, and re-layouts: 9.04 us -> 0.92 us  [one_group(): nodes_here = lax.dynamic_slice_in_dim(page_node, first_page, group_pages, 0)]
    ppermute x4, starting transfers between devices: 18.7 us -> 14 us  [shifted(): lax.ppermute(value, axis, [(source, source + steps) for source in range(f...]
    another operation x3 -> x4, local copies, waits for them, and re-layouts: 0.94 us -> 5.44 us  [the longest x1 5.15 us: local(): jnp.stack([kv_pages] * lax.axis_size('blk'))]
  transfers between devices with their start and end apart: 6 -> 6, of which waited for: 2 -> 3; matrix products, arithmetic and copies ran while one was open for 6% -> 1% of each run, Pallas kernels for 0% -> 0%
where the time goes in v1:
time: 303 us; the launch traced here: 302 us
  waiting for transfers between devices  189 us (62%)
  local copies, waits for them, and re-layouts  35.2 us (12%)
  starting transfers between devices  32 us (11%)
  matrix products  17.8 us (6%)
  between operations  13.8 us (5%)
  other arithmetic  12.7 us (4%)
    ppermute x4, waiting for transfers between devices, shifted(): lax.ppermute(value, axis, [(source, source + steps) for source in range(f...  137 us
    reduce_scatter x1, waiting for transfers between devices, local(): lax.psum_scatter(partial_out, 'head', scatter_dimension=1, tiled=True)  51.7 us
    all_to_all x1, starting transfers between devices, local(): lax.all_to_all(jnp.stack([kv_pages] * lax.axis_size('blk')), 'blk', 0, 0)  17.9 us
    ppermute x4, starting transfers between devices, shifted(): lax.ppermute(value, axis, [(source, source + steps) for source in range(f...  14 us
    dynamic_slice x12, local copies, waits for them, and re-layouts, one_group(): lax.dynamic_slice_in_dim(shard_pages, first_page, group_pages, 1)  13 us
    and x24, local copies, waits for them, and re-layouts, page_mask(): node_hit[:, :, None] & slot_live[None, :, :]  9.92 us
    dot_general x13, matrix products, fold_keys(): jnp.einsum('khrn,knd->khrd', weights.astype(jnp.bfloat16), values, prefer...  8.64 us
    dot_general x13, matrix products, fold_keys(): jnp.einsum('rkhd,knd->khrn', q_rot, key_rows, preferred_element_type=jnp....  7.2 us
  transfers between devices with their start and end apart: 6, of which 3 were waited for; matrix products, arithmetic and copies ran while one was open for 1% of the time, Pallas kernels for 0%

profile of v1, /device:TPU:8, one launch (start us, length us, event | category | flops | bytes accessed | tf_op | source)
XLA Modules:
  0.0 301.7 jit_solution(8424905000816628908)
XLA Ops:
  6.5 5.1 %stack.5 = bf16[128,1,3,64,128]{4,3,2,1,0:T(8,128)(2,1)} broadcast(bf16[3,64,128]{2,1,0:T(8,128)(2,1)} %bitcast.119), dimensions={2,3,4} | broadcast | bytes 6340608 | tf_op jit(solution)/shard_map/stack | solution.py:161
  11.8 17.9 %all-to-all-start = ((bf16[128,1,3,64,128]{4,3,2,1,0:T(8,128)(2,1)}), bf16[128,1,3,64,128]{4,3,2,1,0:T(8,128)(2,1)}, u32[]{:S(2)}, u32[]{:S(2)}) async-start(bf16[128,1,3,64,128]{4,3,2,1,0:T(8,128)(2,1)} %stack.5), calls=%async_computation | async-start | bytes 12582912 | tf_op jit(solution)/shard_map/all_to_all | solution.py:161
  32.3 4.3 %collective-permute-start = (bf16[64,1,128]{2,0,1:T(8,128)(2,1)S(1)}, bf16[64,1,128]{2,0,1:T(8,128)(2,1)S(1)}, u32[]{:S(2)}, u32[]{:S(2)}) collective-permute-start(bf16[64,1,128]{2,0,1:T(8,128)(2,1)S(1)} %pad_maximum_fusion.1), channel_id=1, source_target_pairs={{0,4},{1,5},{2,6},{3,7},{4,8},{5,9},{6,10},{7,11},{8,12},{9,13},{1... | collective-permute-start | bytes 49160 | tf_op jit(solution)/shard_map/ppermute | solution.py:18
  36.6 2.9 collective-permute-start.1
  39.5 4.6 %collective-permute-start.2 = (bf16[64,1,128]{2,0,1:T(8,128)(2,1)S(1)}, bf16[64,1,128]{2,0,1:T(8,128)(2,1)S(1)}, u32[]{:S(2)}, u32[]{:S(2)}) collective-permute-start(bf16[64,1,128]{2,0,1:T(8,128)(2,1)S(1)} %pad_maximum_fusion.1), channel_id=1, source_target_pairs={{0,2},{1,3},{2,4},{3,5},{4,6},{5,7},{6,8},{7,9},{8,10},{9,11},{10,... | collective-permute-start | bytes 49160 | tf_op jit(solution)/shard_map/ppermute | solution.py:18
  44.1 2.3 collective-permute-start.3
  47.6 136.8 %collective-permute-done = bf16[64,1,128]{2,0,1:T(8,128)(2,1)S(1)} collective-permute-done((bf16[64,1,128]{2,0,1:T(8,128)(2,1)S(1)}, bf16[64,1,128]{2,0,1:T(8,128)(2,1)S(1)}, u32[]{:S(2)}, u32[]{:S(2)}) %collective-permute-start) | collective-permute-done | bytes 16416 | tf_op jit(solution)/shard_map/ppermute | solution.py:18
  185.4 0.8 all-to-all-done
  186.2 54.0 %while.17 = (s32[]{:T(128)}, f32[1,4,64]{2,1,0:T(4,128)S(1)}, f32[1,4,64]{2,1,0:T(4,128)S(1)}, f32[1,4,64,64]{3,2,1,0:T(8,128)S(1)}, s32[64,3]{0,1:T(4,128)S(1)}...) while((s32[]{:T(128)}, f32[1,4,64]{2,1,0:T(4,128)S(1)}, ...), condition=%wide.region_15.16_spmd, body=%wide.region_11.15_spmd.sunk | while | flops 139113216 | bytes 9696951 | solution.py:175
  187.7 1.1 constant_dynamic-slice_fusion.2
  192.2 1.1 constant_dynamic-slice_fusion.2
  196.7 1.1 constant_dynamic-slice_fusion.2
  201.3 1.1 constant_dynamic-slice_fusion.2
  205.8 1.1 constant_dynamic-slice_fusion.2
  210.3 1.1 constant_dynamic-slice_fusion.2
  214.7 1.1 constant_dynamic-slice_fusion.2
  219.2 1.1 constant_dynamic-slice_fusion.2
  223.7 1.1 constant_dynamic-slice_fusion.2
  228.2 1.1 constant_dynamic-slice_fusion.2
  232.7 1.1 constant_dynamic-slice_fusion.2
  237.2 1.1 constant_dynamic-slice_fusion.2
  240.5 1.1 fusion.48
  241.6 51.7 %reduce-scatter.2.cloned.1.call-done = f32[64,512]{1,0:T(8,128)} async-done(((f32[64,2048]{1,0:T(8,128)}), f32[64,512]{1,0:T(8,128)}) %reduce-scatter.2.cloned.1.call-update) | async-done | bytes 131088 | tf_op jit(solution)/shard_map/reduce_scatter | solution.py:182
  293.3 1.5 convert_element_type.84
  (291 shorter events, 45.0 us)
Async XLA Ops:
  6.5 233.9 %copy-start = (bf16[256,2048]{1,0:T(8,128)(2,1)S(1)}, bf16[256,2048]{1,0:T(8,128)(2,1)}, u32[]{:S(2)}) copy-start(bf16[256,2048]{1,0:T(8,128)(2,1)} %param.17) | copy-start | bytes 3145732
  11.7 18.1 %copy-start.5 = (s32[64]{0:T(128)S(1)}, s32[64]{0:T(128)}, u32[]{:S(2)}) copy-start(s32[64]{0:T(128)} %param.21) | copy-start | bytes 772
  11.7 18.6 %copy-start.6 = (s32[64]{0:T(128)S(1)}, s32[64]{0:T(128)}, u32[]{:S(2)}) copy-start(s32[64]{0:T(128)} %param.22) | copy-start | bytes 772
  11.7 18.8 %copy-start.9 = (s32[64]{0:T(128)S(1)}, s32[64]{0:T(128)}, u32[]{:S(2)}) copy-start(s32[64]{0:T(128)} %param.23) | copy-start | bytes 772
  11.7 19.0 %copy-start.3 = (s32[384]{0:T(512)S(1)}, s32[384]{0:T(512)}, u32[]{:S(2)}) copy-start(s32[384]{0:T(512)} %param.20) | copy-start | bytes 4612
  11.7 19.0 %copy-start.4 = (s32[384]{0:T(512)S(1)}, s32[384]{0:T(512)}, u32[]{:S(2)}) copy-start(s32[384]{0:T(512)} %param.19) | copy-start | bytes 4612
  11.7 19.4 %copy-start.1 = (bf16[64,2048]{1,0:T(8,128)(2,1)S(1)}, bf16[64,2048]{1,0:T(8,128)(2,1)}, u32[]{:S(2)}) copy-start(bf16[64,2048]{1,0:T(8,128)(2,1)} %param.13) | copy-start | bytes 786436
  11.7 19.5 %copy-start.7 = (bf16[2048,64]{0,1:T(8,128)(2,1)S(1)}, bf16[2048,64]{0,1:T(8,128)(2,1)}, u32[]{:S(2)}) copy-start(bf16[2048,64]{0,1:T(8,128)(2,1)} %param.15) | copy-start | bytes 786436
  11.7 20.2 %copy-start.8 = (bf16[2048,64]{0,1:T(8,128)(2,1)S(1)}, bf16[2048,64]{0,1:T(8,128)(2,1)}, u32[]{:S(2)}) copy-start(bf16[2048,64]{0,1:T(8,128)(2,1)} %param.16) | copy-start | bytes 786436
  11.7 34.6 %copy-start.2 = (bf16[2048,256]{1,0:T(8,128)(2,1)S(1)}, bf16[2048,256]{1,0:T(8,128)(2,1)}, u32[]{:S(2)}) copy-start(bf16[2048,256]{1,0:T(8,128)(2,1)} %param.14) | copy-start | bytes 3145732
  11.8 174.4 %all-to-all-start = ((bf16[128,1,3,64,128]{4,3,2,1,0:T(8,128)(2,1)}), bf16[128,1,3,64,128]{4,3,2,1,0:T(8,128)(2,1)}, u32[]{:S(2)}, u32[]{:S(2)}) async-start(bf16[128,1,3,64,128]{4,3,2,1,0:T(8,128)(2,1)} %stack.5), calls=%async_computation | async-start | bytes 12582912 | tf_op jit(solution)/shard_map/all_to_all | solution.py:161
  29.7 263.6 %reduce-scatter.2.cloned.1.call-start = ((), (), s32[]{:S(2)}) async-start(), calls=%async_computation.2 | async-start | bytes 655360 | tf_op jit(solution)/shard_map/reduce_scatter | solution.py:182
  32.3 152.1 %collective-permute-start = (bf16[64,1,128]{2,0,1:T(8,128)(2,1)S(1)}, bf16[64,1,128]{2,0,1:T(8,128)(2,1)S(1)}, u32[]{:S(2)}, u32[]{:S(2)}) collective-permute-start(bf16[64,1,128]{2,0,1:T(8,128)(2,1)S(1)} %pad_maximum_fusion.1), channel_id=1, source_target_pairs={{0,4},{1,5},{2,6},{3,7},{4,8},{5,9},{6,10},{7,11},{8,12},{9,13},{1... | collective-permute-start | bytes 49160 | tf_op jit(solution)/shard_map/ppermute | solution.py:18
  36.6 147.8 %collective-permute-start.1 = (bf16[64,1,128]{2,0,1:T(8,128)(2,1)S(1)}, bf16[64,1,128]{2,0,1:T(8,128)(2,1)S(1)}, u32[]{:S(2)}, u32[]{:S(2)}) collective-permute-start(bf16[64,1,128]{2,0,1:T(8,128)(2,1)S(1)} %pad_maximum_fusion.1), channel_id=1, source_target_pairs={{0,3},{1,4},{2,5},{3,6},{4,7},{5,8},{6,9},{7,10},{8,11},{9,12},{10... | collective-permute-start | bytes 49160 | tf_op jit(solution)/shard_map/ppermute | solution.py:18
  39.5 145.0 %collective-permute-start.2 = (bf16[64,1,128]{2,0,1:T(8,128)(2,1)S(1)}, bf16[64,1,128]{2,0,1:T(8,128)(2,1)S(1)}, u32[]{:S(2)}, u32[]{:S(2)}) collective-permute-start(bf16[64,1,128]{2,0,1:T(8,128)(2,1)S(1)} %pad_maximum_fusion.1), channel_id=1, source_target_pairs={{0,2},{1,3},{2,4},{3,5},{4,6},{5,7},{6,8},{7,9},{8,10},{9,11},{10,... | collective-permute-start | bytes 49160 | tf_op jit(solution)/shard_map/ppermute | solution.py:18
  44.1 140.4 %collective-permute-start.3 = (bf16[64,1,128]{2,0,1:T(8,128)(2,1)S(1)}, bf16[64,1,128]{2,0,1:T(8,128)(2,1)S(1)}, u32[]{:S(2)}, u32[]{:S(2)}) collective-permute-start(bf16[64,1,128]{2,0,1:T(8,128)(2,1)S(1)} %pad_maximum_fusion.1), channel_id=1, source_target_pairs={{0,1},{1,2},{2,3},{3,4},{4,5},{5,6},{6,7},{7,8},{8,9},{9,10},{10,1... | collective-permute-start | bytes 49160 | tf_op jit(solution)/shard_map/ppermute | solution.py:18
Sparse Core Ops, SparseCore 0:
  241.7 51.5 reduce-scatter.1
